TPU v7x, 32 devices: a whole 2x2x4 slice. The times are simulated.
32 devices in a mesh: row: 2 (over y), col: 8 (over z, core), orient: 2 (over x).
Axes of the slice: x: 2, y: 2, z: 4, core: 2. Of those that a mesh axis runs over, the one named last changes fastest.
Arguments:
- noise: float32 [2, 4096, 4096], P(None, ('row', 'col')), may hold values from -6 to 6
- elevation_library: float32 [16, 128, 128], replicated, may hold values from 0.25 to 1
- tile_choice_index: int32 [32, 32], P('row', 'col'), may hold values from 0 to 15
- family_heading_index: int32 [8], P('orient'), may hold values from 0 to 35
- family_extent_index: int32 [8], P('orient'), may hold values from 0 to 3
Outputs:
- safety_min: float32 [4096, 4096], P('row', ('col', 'orient'))
All inputs are finite; a program needn't handle non-finite values.
Results may differ from a plain program's by a relative error of at most 0.0005.
Values may be sent and summed in bfloat16 or wider, within the bound.
A program may use at most 256 MiB of HBM per device.

v0:
```python
import math
import jax
import jax.numpy as jnp
from jax import lax
from jax.sharding import PartitionSpec as P

R = 8
N_AZ = 36
NSIZE = 4
nugget_share = 0.3
peak_share = 1024.0 / (2.0 * math.pi)
cutoff_ratio = 32.0


def extended(cells, sides, width):
    for axis, dim in sides:
        count = lax.axis_size(axis)
        ends = count - 1
        head = lax.slice_in_dim(cells, 0, width, axis=dim)
        tail = lax.slice_in_dim(cells, cells.shape[dim] - width, cells.shape[dim], axis=dim)
        cells = jnp.concatenate(
            [
                lax.ppermute(tail, axis, [(i, (i + 1) % count) for i in range(ends)]),
                cells,
                lax.ppermute(head, axis, [((i + 1) % count, i) for i in range(ends)]),
            ],
            axis=dim,
        )
    return cells


def partner(x, axis, bit):
    return lax.ppermute(x, axis, [(i, i ^ 1 << bit) for i in range(lax.axis_size(axis))])


def amplitude(u_index, v_index, side_cells):
    wrap_u = jnp.minimum(u_index, side_cells - u_index).astype(jnp.float32)
    wrap_v = jnp.minimum(v_index, side_cells - v_index).astype(jnp.float32)
    cutoff = side_cells / cutoff_ratio
    scaled_u = wrap_u / cutoff
    scaled_v = wrap_v / cutoff
    grown = 1.0 + scaled_u * scaled_u + scaled_v * scaled_v
    spectrum = nugget_share + peak_share / (grown * jnp.sqrt(grown))
    return jnp.sqrt(spectrum) / side_cells


def ellipsoid(offset_u, offset_v, azimuth, size_index):
    heading = azimuth.astype(jnp.float32) * (math.pi / N_AZ)
    semi_axis = R * (size_index.astype(jnp.float32) + (1 + NSIZE)) / (2 * NSIZE)
    across = 0.6 * semi_axis
    slip_depth = 0.3 * semi_axis
    along = offset_u * jnp.cos(heading) + offset_v * jnp.sin(heading)
    lateral = offset_v * jnp.cos(heading) - offset_u * jnp.sin(heading)
    along_part = along / semi_axis
    lateral_part = lateral / across
    inside = 1.0 - along_part * along_part - lateral_part * lateral_part
    height = slip_depth * jnp.sqrt(jnp.maximum(inside, 0.0))
    base_share = jnp.clip(4.0 * inside, 0.0, 1.0)
    return (height, base_share)


def angle_table(row_count, col_count, period):
    left_index = lax.broadcasted_iota(jnp.int32, (row_count, col_count), 0)
    right_index = lax.broadcasted_iota(jnp.int32, (row_count, col_count), 1)
    phase_step = left_index * right_index % period
    angles = phase_step.astype(jnp.float32) * (2.0 * math.pi / period)
    return (jnp.cos(angles), jnp.sin(angles))


def transform_last(real_part, imag_part):
    length = real_part.shape[-1]
    inner_size = 128
    outer_size = length // inner_size
    leading = real_part.shape[:-1]
    real_in = real_part.reshape(leading + (outer_size, inner_size))
    imag_in = imag_part.reshape(leading + (outer_size, inner_size))
    highest = lax.Precision.HIGHEST
    outer_cos, outer_sin = angle_table(outer_size, outer_size, outer_size)
    real_mid = jnp.einsum("...pq,pk->...kq", real_in, outer_cos, precision=highest) + jnp.einsum(
        "...pq,pk->...kq", imag_in, outer_sin, precision=highest
    )
    imag_mid = jnp.einsum("...pq,pk->...kq", imag_in, outer_cos, precision=highest) - jnp.einsum(
        "...pq,pk->...kq", real_in, outer_sin, precision=highest
    )
    twist_cos, twist_sin = angle_table(outer_size, inner_size, length)
    real_twist = real_mid * twist_cos + imag_mid * twist_sin
    imag_twist = imag_mid * twist_cos - real_mid * twist_sin
    inner_cos, inner_sin = angle_table(inner_size, inner_size, inner_size)
    real_out = jnp.einsum("...kq,ql->...kl", real_twist, inner_cos, precision=highest) + jnp.einsum(
        "...kq,ql->...kl", imag_twist, inner_sin, precision=highest
    )
    imag_out = jnp.einsum("...kq,ql->...kl", imag_twist, inner_cos, precision=highest) - jnp.einsum(
        "...kq,ql->...kl", real_twist, inner_sin, precision=highest
    )
    real_out = jnp.swapaxes(real_out, -1, -2).reshape(leading + (length,))
    imag_out = jnp.swapaxes(imag_out, -1, -2).reshape(leading + (length,))
    return (real_out, imag_out)


def body(noise, elevation_library, tile_choice_index, family_heading_index, family_extent_index):
    line_count = noise.shape[1]
    side_cells = noise.shape[2]
    first_line = lax.axis_index(("row", "col")) * line_count
    v_index = first_line + lax.broadcasted_iota(jnp.int32, (line_count, side_cells), 0)
    u_index = lax.broadcasted_iota(jnp.int32, (line_count, side_cells), 1)
    amplitudes = amplitude(u_index, v_index, side_cells)
    real_part, imag_part = transform_last(noise[0] * amplitudes, noise[1] * amplitudes)
    spectrum = jnp.stack([real_part, imag_part])
    transposed = lax.all_to_all(
        spectrum.astype(jnp.bfloat16), ("row", "col"), split_axis=2, concat_axis=1, tiled=True
    ).astype(spectrum.dtype)
    turned = jnp.swapaxes(transposed, 1, 2)
    field_re, field_im = transform_last(turned[0], turned[1])
    fields = lax.all_to_all(
        jnp.stack([field_re, field_im]).astype(jnp.bfloat16),
        "col",
        split_axis=2,
        concat_axis=1,
        tiled=True,
    ).astype(jnp.float32)
    window_rows = fields.shape[1]
    window_columns = fields.shape[2]
    elevation_tiles = jnp.take(elevation_library, tile_choice_index, axis=0)
    slope_tangents = elevation_tiles.transpose(0, 2, 1, 3).reshape(window_rows, window_columns)
    secant = jnp.sqrt(1.0 + slope_tangents * slope_tangents)
    cohesion = 0.5 * jnp.exp(0.4 * fields[0])
    friction = 0.6 * jnp.exp(0.25 * fields[1])
    column_terms = jnp.stack(
        [cohesion * secant, friction / secant, slope_tangents / secant]
    ).astype(jnp.bfloat16)
    padded = extended(column_terms, (("row", 1), ("col", 2)), R)
    tile_width = min(128, window_columns)
    tile_count = window_columns // tile_width
    strip_span = tile_width + 2 * R
    strips = jnp.stack(
        [
            padded[:, :, tile_index * tile_width : tile_index * tile_width + strip_span]
            for tile_index in range(tile_count)
        ],
        axis=2,
    )
    kernel_width = 2 * R + 1
    shift_index = lax.broadcasted_iota(jnp.int32, (kernel_width, strip_span, tile_width), 0)
    strip_index = lax.broadcasted_iota(jnp.int32, (kernel_width, strip_span, tile_width), 1)
    out_index = lax.broadcasted_iota(jnp.int32, (kernel_width, strip_span, tile_width), 2)
    column_gap = strip_index - out_index
    offset_u = (shift_index - R).astype(jnp.float32)
    offset_v = (column_gap - R).astype(jnp.float32)
    inside_band = (column_gap >= 0) & (column_gap <= 2 * R)
    height, base_share = ellipsoid(
        offset_u[None],
        offset_v[None],
        family_heading_index[:, None, None, None],
        family_extent_index[:, None, None, None],
    )
    band_height = jnp.where(inside_band[None], height, 0.0).astype(jnp.bfloat16)
    band_share = jnp.where(inside_band[None], base_share, 0.0).astype(jnp.bfloat16)
    shifted = jnp.stack(
        [strips[:, row_shift : row_shift + window_rows] for row_shift in range(kernel_width)],
        axis=1,
    )
    resist_kernel = jnp.stack([band_share, band_height])
    resisting = jnp.einsum(
        "csxti,cfsio->fxto", shifted[0:2], resist_kernel, preferred_element_type=jnp.float32
    )
    driving = jnp.einsum(
        "sxti,fsio->fxto", shifted[2], band_height, preferred_element_type=jnp.float32
    )
    safety = resisting / driving
    family_low = jnp.min(safety, axis=0).reshape(window_rows, window_columns)
    half_width = window_columns // 2
    side_index = lax.axis_index("orient")
    own_half = lax.dynamic_slice_in_dim(family_low, side_index * half_width, half_width, 1)
    other_half = lax.dynamic_slice_in_dim(family_low, (1 - side_index) * half_width, half_width, 1)
    partner_half = partner(other_half, "orient", 0)
    return jnp.minimum(own_half, partner_half)


def solution(mesh):
    placed = (P(None, ("row", "col"), None), P(), P("row", "col"), P("orient"), P("orient"))
    return jax.shard_map(
        body, mesh=mesh, in_specs=placed, out_specs=P("row", ("col", "orient")), check_vma=False
    )
```

profile of v0, /device:TPU:0, one launch (start us, length us, event | category | flops | bytes accessed | tf_op | source)
XLA Modules:
  0.0 706.0 jit_solution(4212948183642729390)
XLA Ops:
  33.8 7.0 fusion.40
  48.7 6.8 fusion.61
  57.0 25.5 %copy.105 = bf16[2,256,4096]{1,0,2:T(2,128)(2,1)S(1)} copy(bf16[2,256,4096]{1,2,0:T(8,128)(2,1)S(1)} %pad_maximum_fusion.2) | data formatting | bytes 8388608 | tf_op jit(solution)/shard_map/stack | solution.py:108
  82.5 99.9 %all_to_all.27 = bf16[2,256,4096]{1,0,2:T(2,128)(2,1)S(1)} all-to-all(bf16[2,256,4096]{1,0,2:T(2,128)(2,1)S(1)} %copy.105), channel_id=1, replica_groups=mesh['row'=2,'col'=8,'orient'=2] {'row','col'}, dimensions={2} | all-to-all | bytes 8388608 | tf_op jit(solution)/shard_map/all_to_all | solution.py:109
  216.7 6.8 fusion.34
  223.5 6.8 fusion.32
  230.3 7.2 %fusion.62 = bf16[256,128,32]{0,1,2:T(8,128)(2,1)S(1)} fusion(f32[256,32,128]{0,2,1:T(8,128)S(1)} %fusion.34, f32[256,32,128]{2,1,0:T(8,128)S(1)} %get-tuple-element.5), kind=kOutput, calls=%fused_computation.116 | convolution fusion | flops 1612939264 | bytes 10485760 | tf_op jit(solution)/shard_map/...kq,ql->...kl/dot_general | solution.py:89
  238.7 6.7 fusion.63
  247.0 27.2 %copy.116 = bf16[2,256,4096]{1,0,2:T(2,128)(2,1)} copy(bf16[2,256,4096]{1,2,0:T(8,128)(2,1)S(1)} %pad_maximum_fusion.3) | data formatting | bytes 8388608 | tf_op jit(solution)/shard_map/stack | solution.py:115
  298.7 74.4 %all-to-all-done.1 = bf16[2,256,4096]{1,0,2:T(2,128)(2,1)} async-done(((bf16[2,256,4096]{1,0,2:T(2,128)(2,1)}), bf16[2,256,4096]{1,0,2:T(2,128)(2,1)}, u32[]{:S(2)}, u32[]{:S(2)}) %all-to-all-start.1) | async-done | bytes 4194336 | tf_op jit(solution)/shard_map/all_to_all | solution.py:114
  412.2 12.7 %concatenate.10 = bf16[3,2064,512]{1,2,0:T(8,128)(2,1)} concatenate(bf16[3,8,512]{1,2,0:T(8,128)(2,1)} %copy-done.11, bf16[3,2048,512]{1,2,0:T(8,128)(2,1)} %copy-done.2, bf16[3,8,512]{1,2,0:T(8,128)(2,1)} %collective-permute-done.1), dimensions={1} | concatenate | bytes 12681216 | tf_op jit(solution)/shard_map/concatenate | solution.py:21
  444.1 6.7 fusion.18
  464.2 6.9 fusion.15
  471.1 6.7 fusion.14
  484.5 6.9 fusion.12
  498.1 6.7 fusion.10
  504.8 7.0 fusion.9
  511.9 6.7 fusion.8
  525.2 6.8 fusion.6
  532.1 6.7 fusion.5
  538.8 6.7 fusion.4
  552.2 51.8 %fusion = f32[4,128,2048,4,1,1]{2,1,5,4,3,0:T(8,128)} fusion(bf16[3,17,2048,4,144]{2,4,1,0,3:T(8,128)(2,1)} %fusion.3, bf16[2,4,17,144,128,1]{4,3,2,0,5,1:T(8,128)(2,1)} %maximum_bitcast_fusion.4), kind=kOutput, calls=%fused_computation.2 | convolution fusion | flops 41070624768 | bytes 102006784 | tf_op jit(solution)/shard_map/csxti,cfsio->fxto/dot_general | solution.py:163
  604.1 42.4 %fusion.2 = f32[128,2048,4]{1,0,2:T(8,128)} fusion(f32[4,128,2048,4,1,1]{2,1,5,4,3,0:T(8,128)} %fusion, bf16[3,17,2048,4,144]{2,4,1,0,3:T(8,128)(2,1)} %fusion.3, f32[4]{0:T(128)S(1)} %copy-done.16, f32[4]{0:T(128)S(1)} %copy-done.14, f32[4]{0:T(128)S(1)} %copy-done.20, f32[17,144,128]{2,1,0:T(8,128)S(1)} %copy-done.8, f32[4]{0:T(128)S(1)} %copy-done.22, ...), kind=kOutput, calls=%fused_computation.6 | convolution fusion | flops 20562706432 | bytes 62646420 | tf_op jit(solution)/shard_map/sxti,fsio->fxto/dot_general | solution.py:166
  656.6 45.4 %collective-permute-done.4 = f32[2048,256]{1,0:T(8,128)} collective-permute-done((f32[2048,256]{1,0:T(8,128)}, f32[2048,256]{1,0:T(8,128)}, u32[]{:S(2)}, u32[]{:S(2)}) %collective-permute-start.4) | collective-permute-done | bytes 2097184 | tf_op jit(solution)/shard_map/ppermute | solution.py:33
  (129 shorter events, 216.5 us)
Async XLA Ops:
  0.0 279.3 %copy-start = (f32[16,128,128]{2,1,0:T(8,128)S(1)}, f32[16,128,128]{2,1,0:T(8,128)}, u32[]{:S(2)}) copy-start(f32[16,128,128]{2,1,0:T(8,128)} %param.6) | copy-start | bytes 3145732
  274.2 98.9 %all-to-all-start.1 = ((bf16[2,256,4096]{1,0,2:T(2,128)(2,1)}), bf16[2,256,4096]{1,0,2:T(2,128)(2,1)}, u32[]{:S(2)}, u32[]{:S(2)}) async-start(bf16[2,256,4096]{1,0,2:T(2,128)(2,1)} %copy.116), calls=%async_computation.1 | async-start | bytes 8388608 | tf_op jit(solution)/shard_map/all_to_all | solution.py:114
  297.2 103.9 %copy-start.23 = (f32[17]{0:T(128)}, f32[17]{0:T(128)S(1)}, u32[]{:S(2)}) copy-start(f32[17]{0:T(128)S(1)} %add_convert_fusion.3) | copy-start | bytes 208
  297.3 103.8 %copy-start.9 = (pred[17,144,128]{2,1,0:T(8,128)(4,1)}, pred[17,144,128]{2,1,0:T(8,128)(4,1)S(1)}, u32[]{:S(2)}) copy-start(pred[17,144,128]{2,1,0:T(8,128)(4,1)S(1)} %fusion.76) | copy-start | bytes 940036
  298.6 102.5 %copy-start.13 = (f32[4]{0:T(128)}, f32[4]{0:T(128)S(1)}, u32[]{:S(2)}) copy-start(f32[4]{0:T(128)S(1)} %get-tuple-element.34) | copy-start | bytes 52
  298.6 102.5 %copy-start.15 = (f32[4]{0:T(128)}, f32[4]{0:T(128)S(1)}, u32[]{:S(2)}) copy-start(f32[4]{0:T(128)S(1)} %get-tuple-element.35) | copy-start | bytes 52
  298.6 102.5 %copy-start.17 = (f32[4]{0:T(128)}, f32[4]{0:T(128)S(1)}, u32[]{:S(2)}) copy-start(f32[4]{0:T(128)S(1)} %get-tuple-element.36) | copy-start | bytes 52
  298.6 102.5 %copy-start.19 = (f32[4]{0:T(128)}, f32[4]{0:T(128)S(1)}, u32[]{:S(2)}) copy-start(f32[4]{0:T(128)S(1)} %get-tuple-element.39) | copy-start | bytes 52
  298.6 102.5 %copy-start.21 = (f32[4]{0:T(128)}, f32[4]{0:T(128)S(1)}, u32[]{:S(2)}) copy-start(f32[4]{0:T(128)S(1)} %get-tuple-element.40) | copy-start | bytes 52
  389.7 11.5 %copy-start.7 = (f32[17,144,128]{2,1,0:T(8,128)S(1)}, f32[17,144,128]{2,1,0:T(8,128)}, u32[]{:S(2)}) copy-start(f32[17,144,128]{2,1,0:T(8,128)} %add_convert_fusion.2) | copy-start | bytes 3760132
  396.4 11.5 %collective-permute-start = (bf16[3,8,512]{1,2,0:T(8,128)(2,1)S(1)}, bf16[3,8,512]{1,2,0:T(8,128)(2,1)S(1)}, u32[]{:S(2)}, u32[]{:S(2)}) collective-permute-start(bf16[3,8,512]{1,2,0:T(8,128)(2,1)S(1)} %get-tuple-element.20), channel_id=1, source_target_pairs={{0,16},{1,17},{2,18},{3,19},{4,20},{5,21},{6,22},{7,23},{8,24},{9,... | collective-permute-start | bytes 73736 | tf_op jit(solution)/shard_map/ppermute | solution.py:23
  399.8 12.4 %collective-permute-start.1 = (bf16[3,8,512]{1,2,0:T(8,128)(2,1)S(1)}, bf16[3,8,512]{1,2,0:T(8,128)(2,1)}, u32[]{:S(2)}, u32[]{:S(2)}) collective-permute-start(bf16[3,8,512]{1,2,0:T(8,128)(2,1)S(1)} %get-tuple-element.19), channel_id=1, source_target_pairs={{16,0},{17,1},{18,2},{19,3},{20,4},{21,5},{22,6},{23,7},{24,8},{25... | collective-permute-start | bytes 73736 | tf_op jit(solution)/shard_map/ppermute | solution.py:25
  425.9 7.0 collective-permute-start.2
  427.2 5.7 collective-permute-start.3
  552.2 51.9 %copy-start.8 = (f32[17,144,128]{2,1,0:T(8,128)S(1)}, f32[17,144,128]{2,1,0:T(8,128)}, u32[]{:S(2)}) copy-start(f32[17,144,128]{2,1,0:T(8,128)} %add_convert_fusion.2) | copy-start | bytes 3760132
  552.2 51.9 %copy-start.10 = (pred[17,144,128]{2,1,0:T(8,128)(4,1)S(1)}, pred[17,144,128]{2,1,0:T(8,128)(4,1)}, u32[]{:S(2)}) copy-start(pred[17,144,128]{2,1,0:T(8,128)(4,1)} %copy-done.9) | copy-start | bytes 940036
  552.2 51.9 %copy-start.14 = (f32[4]{0:T(128)S(1)}, f32[4]{0:T(128)}, u32[]{:S(2)}) copy-start(f32[4]{0:T(128)} %copy-done.13) | copy-start | bytes 52
  552.2 51.9 %copy-start.16 = (f32[4]{0:T(128)S(1)}, f32[4]{0:T(128)}, u32[]{:S(2)}) copy-start(f32[4]{0:T(128)} %copy-done.15) | copy-start | bytes 52
  552.2 51.9 %copy-start.18 = (f32[4]{0:T(128)S(1)}, f32[4]{0:T(128)}, u32[]{:S(2)}) copy-start(f32[4]{0:T(128)} %copy-done.17) | copy-start | bytes 52
  552.2 51.9 %copy-start.20 = (f32[4]{0:T(128)S(1)}, f32[4]{0:T(128)}, u32[]{:S(2)}) copy-start(f32[4]{0:T(128)} %copy-done.19) | copy-start | bytes 52
  552.2 51.9 %copy-start.22 = (f32[4]{0:T(128)S(1)}, f32[4]{0:T(128)}, u32[]{:S(2)}) copy-start(f32[4]{0:T(128)} %copy-done.21) | copy-start | bytes 52
  552.2 51.9 %copy-start.24 = (f32[17]{0:T(128)S(1)}, f32[17]{0:T(128)}, u32[]{:S(2)}) copy-start(f32[17]{0:T(128)} %copy-done.23) | copy-start | bytes 208
  653.3 48.7 %collective-permute-start.4 = (f32[2048,256]{1,0:T(8,128)}, f32[2048,256]{1,0:T(8,128)}, u32[]{:S(2)}, u32[]{:S(2)}) collective-permute-start(f32[2048,256]{1,0:T(8,128)} %copy.147), channel_id=1, source_target_pairs={{0,1},{1,0},{2,3},{3,2},{4,5},{5,4},{6,7},{7,6},{8,9},{9,8},{10,11... | collective-permute-start | bytes 6291464 | tf_op jit(solution)/shard_map/ppermute | solution.py:33
  654.8 51.0 %copy-start.1 = (f32[16,128,128]{2,1,0:T(8,128)S(1)}, f32[16,128,128]{2,1,0:T(8,128)}, u32[]{:S(2)}) copy-start(f32[16,128,128]{2,1,0:T(8,128)} %param.6) | copy-start | bytes 3145732
  (9 other events, 32.9 us)
where the time goes:
time: 711 us; the launch traced here: 706 us
  local copies, waits for them, and re-layouts  243 us (34%)
  matrix products  178 us (25%)
  waiting for transfers between devices  125 us (18%)
  blocking collectives  99.9 us (14%)
  other arithmetic  45.5 us (6%)
  starting transfers between devices  13.6 us (2%)
    unnamed x75, local copies, waits for them, and re-layouts  122 us
    all_to_all x1, blocking collectives, body(): lax.all_to_all(spectrum.astype(jnp.bfloat16), ('row', 'col'), split_axis=...  99.9 us
    all_to_all x1, waiting for transfers between devices, body(): lax.all_to_all(jnp.stack([field_re, field_im]).astype(jnp.bfloat16), 'col...  74.4 us
    dot_general x1, matrix products, body(): jnp.einsum('csxti,cfsio->fxto', shifted[0:2], resist_kernel, preferred_el...  51.8 us
    ppermute x1, waiting for transfers between devices, partner(): lax.ppermute(x, axis, [(i, i ^ 1 << bit) for i in range(lax.axis_size(axi...  45.4 us
    dot_general x1, matrix products, body(): jnp.einsum('sxti,fsio->fxto', shifted[2], band_height, preferred_element_...  42.4 us
    another operation x1, local copies, waits for them, and re-layouts, body(): jnp.stack([field_re, field_im]).astype(jnp.bfloat16)  27.2 us
    another operation x1, local copies, waits for them, and re-layouts, body(): spectrum = jnp.stack([real_part, imag_part])  25.5 us
  transfers between devices with their start and end apart: 6, of which 4 were waited for; matrix products, arithmetic and copies ran while one was open for 4% of the time, Pallas kernels for 0%

commit v1 on v0

--- a/solution.py
+++ b/solution.py
@@ -3,6 +3,7 @@
 import jax.numpy as jnp
 from jax import lax
 from jax.sharding import PartitionSpec as P
+from jax.lax import axis_index, axis_size, ppermute
 
 R = 8
 N_AZ = 36
@@ -10,6 +11,37 @@
 nugget_share = 0.3
 peak_share = 1024.0 / (2.0 * math.pi)
 cutoff_ratio = 32.0
+
+
+def scan_results(w_in, where_dim, local_values):
+    left_arr = w_in.shape
+    block_last = w_in.reshape(
+        *left_arr[:where_dim],
+        local_values,
+        left_arr[where_dim] // local_values,
+        *left_arr[where_dim + 1 :]
+    )
+    return jnp.moveaxis(block_last, where_dim, 0)
+
+
+def remake_sums_all(tile_in, d_out):
+    f_now = list(tile_in.shape[1:])
+    f_now[d_out] *= tile_in.shape[0]
+    return jnp.moveaxis(tile_in, 0, d_out).reshape(f_now)
+
+
+def produce_the_knots(obj, axis_name, shard_in, x0):
+    small = axis_size(axis_name)
+    r1, big = (small, axis_index(axis_name))
+    reached = scan_results(obj, shard_in, r1)
+    chunks = [reached[big]]
+    for k0 in range(1, r1):
+        extra = reached[(big + k0) % r1]
+        t_next = ppermute(extra, axis_name, [(hop_no, (hop_no + k0) % r1) for hop_no in range(r1)])
+        chunks.append(t_next)
+    arr_out = jnp.stack(chunks, axis=0)
+    reached = arr_out[(big - jnp.arange(r1)) % r1]
+    return remake_sums_all(reached, x0)
 
 
 def extended(cells, sides, width):
@@ -111,12 +143,8 @@
     ).astype(spectrum.dtype)
     turned = jnp.swapaxes(transposed, 1, 2)
     field_re, field_im = transform_last(turned[0], turned[1])
-    fields = lax.all_to_all(
-        jnp.stack([field_re, field_im]).astype(jnp.bfloat16),
-        "col",
-        split_axis=2,
-        concat_axis=1,
-        tiled=True,
+    fields = produce_the_knots(
+        jnp.stack([field_re, field_im]).astype(jnp.bfloat16), "col", shard_in=2, x0=1
     ).astype(jnp.float32)
     window_rows = fields.shape[1]
     window_columns = fields.shape[2]

time: 711 us -> 698 us (0.982)
  the two profiles are of different devices: /device:TPU:0 before, /device:TPU:24 now
where the time goes in v1:
time: 698 us; the launch traced here: 693 us
  local copies, waits for them, and re-layouts  251 us (36%)
  matrix products  178 us (26%)
  waiting for transfers between devices  170 us (24%)
  other arithmetic  52.9 us (8%)
  starting transfers between devices  39.6 us (6%)
    unnamed x82, local copies, waits for them, and re-layouts  130 us
    all_to_all x1, waiting for transfers between devices, body(): lax.all_to_all(spectrum.astype(jnp.bfloat16), ('row', 'col'), split_axis=...  67 us
    ppermute x7, waiting for transfers between devices, produce_the_knots(): ppermute(extra, axis_name, [(hop_no, (hop_no + k0) % r1) for hop_no in ra...  57.1 us
    dot_general x1, matrix products, body(): jnp.einsum('csxti,cfsio->fxto', shifted[0:2], resist_kernel, preferred_el...  52 us
    ppermute x1, waiting for transfers between devices, partner(): lax.ppermute(x, axis, [(i, i ^ 1 << bit) for i in range(lax.axis_size(axi...  43.9 us
    dot_general x1, matrix products, body(): jnp.einsum('sxti,fsio->fxto', shifted[2], band_height, preferred_element_...  42.4 us
    another operation x1, local copies, waits for them, and re-layouts, body(): spectrum = jnp.stack([real_part, imag_part])  27.5 us
    ppermute x7, starting transfers between devices, produce_the_knots(): ppermute(extra, axis_name, [(hop_no, (hop_no + k0) % r1) for hop_no in ra...  22.8 us
  transfers between devices with their start and end apart: 13, of which 5 were waited for; matrix products, arithmetic and copies ran while one was open for 8% of the time, Pallas kernels for 0%

profile of v1, /device:TPU:24, one launch (start us, length us, event | category | flops | bytes accessed | tf_op | source)
XLA Modules:
  0.0 692.9 jit_solution(16844883480790538151)
XLA Ops:
  33.5 6.8 fusion.38
  56.3 27.5 %copy.121 = bf16[2,256,4096]{1,0,2:T(2,128)(2,1)} copy(bf16[2,256,4096]{1,2,0:T(8,128)(2,1)S(1)} %pad_maximum_fusion.2) | data formatting | bytes 8388608 | tf_op jit(solution)/shard_map/stack | solution.py:140
  110.0 67.0 %all-to-all-done = bf16[2,256,4096]{1,0,2:T(2,128)(2,1)} async-done(((bf16[2,256,4096]{1,0,2:T(2,128)(2,1)}), bf16[2,256,4096]{1,0,2:T(2,128)(2,1)}, u32[]{:S(2)}, u32[]{:S(2)}) %all-to-all-start) | async-done | bytes 4194336 | tf_op jit(solution)/shard_map/all_to_all | solution.py:141
  213.5 7.0 %fusion.30 = f32[256,32,128]{0,2,1:T(8,128)S(1)} fusion(f32[256,32,128]{2,1,0:T(8,128)S(1)} %get-tuple-element.6), kind=kOutput, calls=%fused_computation.97 | convolution fusion | flops 1610842112 | bytes 8388608 | tf_op jit(solution)/shard_map/...kq,ql->...kl/dot_general | solution.py:124
  227.1 7.2 %fusion.61 = bf16[256,128,32]{0,1,2:T(8,128)(2,1)S(1)} fusion(f32[256,32,128]{0,2,1:T(8,128)S(1)} %fusion.30, f32[256,32,128]{2,1,0:T(8,128)S(1)} %get-tuple-element.5), kind=kOutput, calls=%fused_computation.131 | convolution fusion | flops 1612939264 | bytes 10485760 | tf_op jit(solution)/shard_map/...kq,ql->...kl/dot_general | solution.py:124
  235.5 6.8 fusion.60
  272.7 12.6 %collective-permute-start.6 = (bf16[2,256,512]{2,1,0:T(8,128)(2,1)S(1)}, bf16[2,256,512]{2,1,0:T(8,128)(2,1)S(1)}, u32[]{:S(2)}, u32[]{:S(2)}) collective-permute-start(bf16[2,256,512]{2,1,0:T(8,128)(2,1)S(1)} %bitcast.282), channel_id=1, source_target_pairs={{0,14},{2,0},{4,2},{6,4},{8,6},{10,8},{12,10},{14,12},{1,15},{3,1}... | collective-permute-start | bytes 1572872 | tf_op jit(solution)/shard_map/ppermute | solution.py:40
  287.2 43.5 %collective-permute-done.2 = bf16[2,256,512]{2,1,0:T(8,128)(2,1)} collective-permute-done((bf16[2,256,512]{2,1,0:T(8,128)(2,1)}, bf16[2,256,512]{2,1,0:T(8,128)(2,1)}, u32[]{:S(2)}, u32[]{:S(2)}) %collective-permute-start.2) | collective-permute-done | bytes 524320 | tf_op jit(solution)/shard_map/ppermute | solution.py:40
  332.6 13.5 %collective-permute-done.3 = bf16[2,256,512]{2,1,0:T(8,128)(2,1)} collective-permute-done((bf16[2,256,512]{2,1,0:T(8,128)(2,1)}, bf16[2,256,512]{2,1,0:T(8,128)(2,1)}, u32[]{:S(2)}, u32[]{:S(2)}) %collective-permute-start.3) | collective-permute-done | bytes 524320 | tf_op jit(solution)/shard_map/ppermute | solution.py:40
  374.4 7.1 %multiply_convert_fusion.2 = (bf16[1,2048,512]{1,2,0:T(8,128)(2,1)S(1)}, bf16[1,2048,512]{1,2,0:T(8,128)(2,1)S(1)}, bf16[1,2048,512]{1,2,0:T(8,128)(2,1)S(1)}) fusion(f32[1,2048,512]{1,2,0:T(8,128)} %copy.168, f32[1,2048,512]{1,2,0:T(8,128)} %reshape.273, f32[1,2048,512]{1,2,0:T(8,128)} %copy.169), kind=kLoop, calls=%fused_computation.84 | loop fusion | flops 8388608 | bytes 18874368 | tf_op jit(solution)/shard_map/convert.1
  398.8 12.7 %concatenate.12 = bf16[3,2064,512]{1,2,0:T(8,128)(2,1)} concatenate(bf16[3,8,512]{1,2,0:T(8,128)(2,1)} %copy-done.11, bf16[3,2048,512]{1,2,0:T(8,128)(2,1)} %copy-done.2, bf16[3,8,512]{1,2,0:T(8,128)(2,1)} %collective-permute-done.8), dimensions={1} | concatenate | bytes 12681216 | tf_op jit(solution)/shard_map/concatenate | solution.py:53
  439.2 6.7 fusion.17
  452.6 6.8 fusion.15
  459.4 6.7 fusion.14
  466.1 6.7 fusion.13
  472.8 6.9 fusion.12
  486.3 6.7 fusion.10
  493.0 7.0 %fusion.9 = bf16[3,17,2048,4,144]{2,4,1,0,3:T(8,128)(2,1)} fusion(bf16[3,17,2048,4,144]{2,4,1,0,3:T(8,128)(2,1)} %fusion.10, bf16[3,2064,4,144]{1,3,0,2:T(8,128)(2,1)S(1)} %pad_maximum_fusion), kind=kLoop, calls=%fused_computation.39 | loop fusion | bytes 14155776
  500.1 6.7 fusion.8
  513.5 6.9 fusion.6
  520.4 6.7 fusion.5
  540.5 52.0 %fusion = f32[4,128,2048,4,1,1]{2,1,5,4,3,0:T(8,128)} fusion(bf16[3,17,2048,4,144]{2,4,1,0,3:T(8,128)(2,1)} %fusion.3, bf16[2,4,17,144,128,1]{4,3,2,0,5,1:T(8,128)(2,1)} %maximum_bitcast_fusion.4), kind=kOutput, calls=%fused_computation.3 | convolution fusion | flops 41070624768 | bytes 102006784 | tf_op jit(solution)/shard_map/csxti,cfsio->fxto/dot_general | solution.py:191
  592.5 42.4 %fusion.2 = f32[128,2048,4]{1,0,2:T(8,128)} fusion(f32[4,128,2048,4,1,1]{2,1,5,4,3,0:T(8,128)} %fusion, bf16[3,17,2048,4,144]{2,4,1,0,3:T(8,128)(2,1)} %fusion.3, f32[4]{0:T(128)S(1)} %copy-done.16, f32[4]{0:T(128)S(1)} %copy-done.14, f32[4]{0:T(128)S(1)} %copy-done.20, f32[17,144,128]{2,1,0:T(8,128)S(1)} %copy-done.7, f32[4]{0:T(128)S(1)} %copy-done.22, ...), kind=kOutput, calls=%fused_computation.7 | convolution fusion | flops 20562706432 | bytes 62646420 | tf_op jit(solution)/shard_map/sxti,fsio->fxto/dot_general | solution.py:194
  645.0 43.9 %collective-permute-done.11 = f32[2048,256]{1,0:T(8,128)} collective-permute-done((f32[2048,256]{1,0:T(8,128)}, f32[2048,256]{1,0:T(8,128)}, u32[]{:S(2)}, u32[]{:S(2)}) %collective-permute-start.11) | collective-permute-done | bytes 2097184 | tf_op jit(solution)/shard_map/ppermute | solution.py:65
  (160 shorter events, 274.4 us)
Async XLA Ops:
  0.0 90.2 %copy-start = (f32[16,128,128]{2,1,0:T(8,128)S(1)}, f32[16,128,128]{2,1,0:T(8,128)}, u32[]{:S(2)}) copy-start(f32[16,128,128]{2,1,0:T(8,128)} %param.6) | copy-start | bytes 3145732
  83.8 93.2 %all-to-all-start = ((bf16[2,256,4096]{1,0,2:T(2,128)(2,1)}), bf16[2,256,4096]{1,0,2:T(2,128)(2,1)}, u32[]{:S(2)}, u32[]{:S(2)}) async-start(bf16[2,256,4096]{1,0,2:T(2,128)(2,1)} %copy.121), calls=%async_computation | async-start | bytes 8388608 | tf_op jit(solution)/shard_map/all_to_all | solution.py:141
  248.3 22.2 %collective-permute-start = (bf16[2,256,512]{2,1,0:T(8,128)(2,1)}, bf16[2,256,512]{2,1,0:T(8,128)(2,1)}, u32[]{:S(2)}, u32[]{:S(2)}) collective-permute-start(bf16[2,256,512]{2,1,0:T(8,128)(2,1)} %bitcast.283), channel_id=1, source_target_pairs={{0,2},{2,4},{4,6},{6,8},{8,10},{10,12},{12,14},{14,0},{1,3},{3,5},... | collective-permute-start | bytes 1572872 | tf_op jit(solution)/shard_map/ppermute | solution.py:40
  251.7 20.9 %collective-permute-start.1 = (bf16[2,256,512]{2,1,0:T(8,128)(2,1)}, bf16[2,256,512]{2,1,0:T(8,128)(2,1)}, u32[]{:S(2)}, u32[]{:S(2)}) collective-permute-start(bf16[2,256,512]{2,1,0:T(8,128)(2,1)} %bitcast.281), channel_id=1, source_target_pairs={{0,4},{2,6},{4,8},{6,10},{8,12},{10,14},{12,0},{14,2},{1,5},{3,7},... | collective-permute-start | bytes 1572872 | tf_op jit(solution)/shard_map/ppermute | solution.py:40
  255.7 14.3 %copy-start.8 = (bf16[2,256,1,512]{1,3,2,0:T(8,128)(2,1)S(1)}, bf16[2,256,1,512]{1,3,2,0:T(8,128)(2,1)}, u32[]{:S(2)}) copy-start(bf16[2,256,1,512]{1,3,2,0:T(8,128)(2,1)} %get-tuple-element.32) | copy-start | bytes 1572868
  257.0 91.0 %collective-permute-start.4 = (bf16[2,256,512]{2,1,0:T(8,128)(2,1)S(1)}, bf16[2,256,512]{2,1,0:T(8,128)(2,1)S(1)}, u32[]{:S(2)}, u32[]{:S(2)}) collective-permute-start(bf16[2,256,512]{2,1,0:T(8,128)(2,1)S(1)} %bitcast.280), channel_id=1, source_target_pairs={{0,10},{2,12},{4,14},{6,0},{8,2},{10,4},{12,6},{14,8},{1,11},{3,13... | collective-permute-start | bytes 1572872 | tf_op jit(solution)/shard_map/ppermute | solution.py:40
  264.9 65.8 %collective-permute-start.2 = (bf16[2,256,512]{2,1,0:T(8,128)(2,1)}, bf16[2,256,512]{2,1,0:T(8,128)(2,1)}, u32[]{:S(2)}, u32[]{:S(2)}) collective-permute-start(bf16[2,256,512]{2,1,0:T(8,128)(2,1)} %bitcast.285), channel_id=1, source_target_pairs={{0,6},{2,8},{4,10},{6,12},{8,14},{10,0},{12,2},{14,4},{1,7},{3,9},... | collective-permute-start | bytes 1572872 | tf_op jit(solution)/shard_map/ppermute | solution.py:40
  268.0 78.1 %collective-permute-start.3 = (bf16[2,256,512]{2,1,0:T(8,128)(2,1)}, bf16[2,256,512]{2,1,0:T(8,128)(2,1)}, u32[]{:S(2)}, u32[]{:S(2)}) collective-permute-start(bf16[2,256,512]{2,1,0:T(8,128)(2,1)} %bitcast.32), channel_id=1, source_target_pairs={{0,8},{2,10},{4,12},{6,14},{8,0},{10,2},{12,4},{14,6},{1,9},{3,11}... | collective-permute-start | bytes 1572872 | tf_op jit(solution)/shard_map/ppermute | solution.py:40
  270.5 78.3 %collective-permute-start.5 = (bf16[2,256,512]{2,1,0:T(8,128)(2,1)S(1)}, bf16[2,256,512]{2,1,0:T(8,128)(2,1)S(1)}, u32[]{:S(2)}, u32[]{:S(2)}) collective-permute-start(bf16[2,256,512]{2,1,0:T(8,128)(2,1)S(1)} %bitcast.284), channel_id=1, source_target_pairs={{0,12},{2,14},{4,0},{6,2},{8,4},{10,6},{12,8},{14,10},{1,13},{3,15... | collective-permute-start | bytes 1572872 | tf_op jit(solution)/shard_map/ppermute | solution.py:40
  272.7 77.0 %collective-permute-start.6 = (bf16[2,256,512]{2,1,0:T(8,128)(2,1)S(1)}, bf16[2,256,512]{2,1,0:T(8,128)(2,1)S(1)}, u32[]{:S(2)}, u32[]{:S(2)}) collective-permute-start(bf16[2,256,512]{2,1,0:T(8,128)(2,1)S(1)} %bitcast.282), channel_id=1, source_target_pairs={{0,14},{2,0},{4,2},{6,4},{8,6},{10,8},{12,10},{14,12},{1,15},{3,1}... | collective-permute-start | bytes 1572872 | tf_op jit(solution)/shard_map/ppermute | solution.py:40
  385.5 10.5 %collective-permute-start.7 = (bf16[3,8,512]{1,2,0:T(8,128)(2,1)S(1)}, bf16[3,8,512]{1,2,0:T(8,128)(2,1)S(1)}, u32[]{:S(2)}, u32[]{:S(2)}) collective-permute-start(bf16[3,8,512]{1,2,0:T(8,128)(2,1)S(1)} %get-tuple-element.20), channel_id=1, source_target_pairs={{0,16},{1,17},{2,18},{3,19},{4,20},{5,21},{6,22},{7,23},{8,24},{9,... | collective-permute-start | bytes 73736 | tf_op jit(solution)/shard_map/ppermute | solution.py:55
  389.0 9.8 %collective-permute-start.8 = (bf16[3,8,512]{1,2,0:T(8,128)(2,1)S(1)}, bf16[3,8,512]{1,2,0:T(8,128)(2,1)}, u32[]{:S(2)}, u32[]{:S(2)}) collective-permute-start(bf16[3,8,512]{1,2,0:T(8,128)(2,1)S(1)} %get-tuple-element.19), channel_id=1, source_target_pairs={{16,0},{17,1},{18,2},{19,3},{20,4},{21,5},{22,6},{23,7},{24,8},{25... | collective-permute-start | bytes 73736 | tf_op jit(solution)/shard_map/ppermute | solution.py:57
  412.5 8.8 %collective-permute-start.10 = (bf16[3,2064,8]{1,2,0:T(8,128)(2,1)S(1)}, bf16[3,2064,8]{1,2,0:T(8,128)(2,1)S(1)}, u32[]{:S(2)}, u32[]{:S(2)}) collective-permute-start(bf16[3,2064,8]{1,2,0:T(8,128)(2,1)S(1)} %get-tuple-element.18), channel_id=1, source_target_pairs={{2,0},{4,2},{6,4},{8,6},{10,8},{12,10},{14,12},{3,1},{5,3},{7,5},{... | collective-permute-start | bytes 297224 | tf_op jit(solution)/shard_map/ppermute | solution.py:57
  414.4 6.8 collective-permute-start.9
  540.4 52.0 %copy-start.7 = (f32[17,144,128]{2,1,0:T(8,128)S(1)}, f32[17,144,128]{2,1,0:T(8,128)}, u32[]{:S(2)}) copy-start(f32[17,144,128]{2,1,0:T(8,128)} %add_convert_fusion.2) | copy-start | bytes 3760132
  540.4 52.0 %copy-start.10 = (pred[17,144,128]{2,1,0:T(8,128)(4,1)S(1)}, pred[17,144,128]{2,1,0:T(8,128)(4,1)}, u32[]{:S(2)}) copy-start(pred[17,144,128]{2,1,0:T(8,128)(4,1)} %fusion.74) | copy-start | bytes 940036
  540.4 52.0 %copy-start.14 = (f32[4]{0:T(128)S(1)}, f32[4]{0:T(128)}, u32[]{:S(2)}) copy-start(f32[4]{0:T(128)} %get-tuple-element.42) | copy-start | bytes 52
  540.4 52.0 %copy-start.16 = (f32[4]{0:T(128)S(1)}, f32[4]{0:T(128)}, u32[]{:S(2)}) copy-start(f32[4]{0:T(128)} %get-tuple-element.43) | copy-start | bytes 52
  540.4 52.0 %copy-start.18 = (f32[4]{0:T(128)S(1)}, f32[4]{0:T(128)}, u32[]{:S(2)}) copy-start(f32[4]{0:T(128)} %get-tuple-element.44) | copy-start | bytes 52
  540.4 52.0 %copy-start.20 = (f32[4]{0:T(128)S(1)}, f32[4]{0:T(128)}, u32[]{:S(2)}) copy-start(f32[4]{0:T(128)} %get-tuple-element.47) | copy-start | bytes 52
  540.4 52.0 %copy-start.22 = (f32[4]{0:T(128)S(1)}, f32[4]{0:T(128)}, u32[]{:S(2)}) copy-start(f32[4]{0:T(128)} %get-tuple-element.48) | copy-start | bytes 52
  540.5 52.0 %copy-start.24 = (f32[17]{0:T(128)S(1)}, f32[17]{0:T(128)}, u32[]{:S(2)}) copy-start(f32[17]{0:T(128)} %add_convert_fusion.3) | copy-start | bytes 208
  641.7 47.2 %collective-permute-start.11 = (f32[2048,256]{1,0:T(8,128)}, f32[2048,256]{1,0:T(8,128)}, u32[]{:S(2)}, u32[]{:S(2)}) collective-permute-start(f32[2048,256]{1,0:T(8,128)} %copy.171), channel_id=1, source_target_pairs={{0,1},{1,0},{2,3},{3,2},{4,5},{5,4},{6,7},{7,6},{8,9},{9,8},{10,11... | collective-permute-start | bytes 6291464 | tf_op jit(solution)/shard_map/ppermute | solution.py:65
  643.2 49.5 %copy-start.1 = (f32[16,128,128]{2,1,0:T(8,128)S(1)}, f32[16,128,128]{2,1,0:T(8,128)}, u32[]{:S(2)}) copy-start(f32[16,128,128]{2,1,0:T(8,128)} %param.6) | copy-start | bytes 3145732
  (16 other events, 101.2 us)
